TPU v7x, 32 devices: a whole 2x2x4 slice. The times are simulated.
32 devices in a mesh: lon: 8 (over z, y), lat: 4 (over x, core).
Axes of the slice: x: 2, y: 2, z: 4, core: 2. Of those that a mesh axis runs over, the one named last changes fastest.
Arguments:
- tokens: bfloat16 [128, 256, 768], P('lat', 'lon'), may hold values from -6 to 6
- norm_gain: float32 [768], replicated, may hold values from 0.1 to 1.9
- inproj_weight: bfloat16 [768, 1152], P('lat')
- outproj_weight: bfloat16 [384, 768], P('lat'), may hold values from -0.3125 to 0.3125
- merge_gain: float32 [3072], replicated, may hold values from 0.1 to 1.9
- merge_weight: bfloat16 [3072, 768], P('lat'), may hold values from -0.109375 to 0.109375
- ocean_flags: int32 [8, 16], P('lat', 'lon'), may hold values 0 or 1
- fold_partner: int32 [256], P('lon'), may hold values from 0 to 255, as said below
Outputs:
- merged: bfloat16 [64, 128, 768], P('lat', 'lon')
Inputs may be any that keep to these rules, and one draw needn't show every extreme that they name: `fold_partner`: the 32 entries c in [i*32, (i+1)*32) name each column of the block [(256 // 32 - 1 - i)*32, (256 // 32 - i)*32) once.
All inputs are finite; a program needn't handle non-finite values. No bound on the sum of `ocean_flags` on one device may be relied on, other than what follows from the above.
Results may differ from a plain program's by a relative error of at most 0.0063.
Values may be sent and summed in bfloat16 or wider, within the bound.
A program may use at most 64 MiB of HBM per device.

v0:
```python
import jax
import jax.numpy as jnp
from jax import lax
from jax.sharding import PartitionSpec as P

HEADS = 12
HD = 32
WIN = 16


epsilon = 1e-05


def shifted_2(shard, axis, by):
    count = lax.axis_size(axis)
    pairs = [(i, i + by) for i in range(count) if 0 <= i + by < count]
    return lax.ppermute(shard, axis, pairs)


def partner(value, axis, distance):
    mask = 2**distance
    pairs = [(source, source ^ mask) for source in range(lax.axis_size(axis))]
    return lax.ppermute(value, axis, pairs)


def from_behind(value, axis, steps):
    count = lax.axis_size(axis)
    pairs = [(source, (source + steps) % count) for source in range(count)]
    return lax.ppermute(value, axis, pairs)


def layer_norm(values, norm_scale):
    center = values - jnp.mean(values, axis=-1, keepdims=True)
    spread = jnp.mean(center * center, axis=-1, keepdims=True)
    return center * lax.rsqrt(spread + epsilon) * norm_scale


def to_windows(region):
    down_count = region.shape[0] // WIN
    across = region.shape[1] // WIN
    channel = region.shape[2]
    tiled_view = region.reshape(down_count, WIN, across, WIN, channel).transpose(0, 2, 1, 3, 4)
    return tiled_view.reshape(down_count * across, WIN * WIN, channel)


def from_windows(windows, down_count, across):
    channel = windows.shape[-1]
    tiled_view = windows.reshape(down_count, across, WIN, WIN, channel).transpose(0, 2, 1, 3, 4)
    return tiled_view.reshape(down_count * WIN, across * WIN, channel)


def window_branch(window, in_weight, out_weight, norm_scale):
    head_width = HEADS * HD
    normed = layer_norm(window.astype(jnp.float32), norm_scale).astype(jnp.bfloat16)
    packed = jnp.dot(normed, in_weight, preferred_element_type=jnp.float32).astype(jnp.bfloat16)
    queries = packed[:, :head_width].reshape(-1, HEADS, HD)
    key_cols = packed[:, head_width : 2 * head_width].reshape(-1, HEADS, HD)
    value_cols = packed[:, 2 * head_width :].reshape(-1, HEADS, HD)
    scores = jnp.einsum(
        "qhd,khd->hqk", queries, key_cols, preferred_element_type=jnp.float32
    ) * HD ** (-0.5)
    highest = jnp.max(scores, axis=-1, keepdims=True)
    lifted = jnp.exp(scores - highest)
    weights = (lifted / jnp.sum(lifted, axis=-1, keepdims=True)).astype(jnp.bfloat16)
    mixed_heads = jnp.einsum(
        "hqk,khd->qhd", weights, value_cols, preferred_element_type=jnp.float32
    )
    mixed_heads = mixed_heads.reshape(-1, head_width).astype(jnp.bfloat16)
    return jnp.dot(mixed_heads, out_weight, preferred_element_type=jnp.float32)


def run_windows(region, flags, in_weight, out_weight, norm_scale):
    down_count = region.shape[0] // WIN
    across = region.shape[1] // WIN
    windows = to_windows(region)

    def one_window(window_item):
        window, ocean_flag = window_item
        computed = window_branch(window, in_weight, out_weight, norm_scale)
        branch = jnp.where(ocean_flag > 0, computed, jnp.zeros_like(computed))
        return (window.astype(jnp.float32) + branch).astype(jnp.bfloat16)

    results = lax.map(one_window, (windows, flags.reshape(-1)))
    return from_windows(results, down_count, across)


def per_device(
    tokens,
    norm_gain,
    inproj_weight,
    outproj_weight,
    merge_gain,
    merge_weight,
    ocean_flags,
    fold_partner,
):
    height = tokens.shape[0]
    breadth = tokens.shape[1]
    half_win = WIN // 2
    in_weight, out_weight = (
        lax.all_gather(inproj_weight, "lat", axis=0, tiled=True),
        lax.all_gather(outproj_weight, "lat", axis=0, tiled=True),
    )
    from_north = shifted_2(tokens[:half_win], "lat", -1)
    mirrored = tokens[height - half_win :][::-1]
    lon_count = lax.axis_size("lon")
    bit_total = lon_count.bit_length() - 1
    for bit_number in range(bit_total):
        mirrored = partner(mirrored, "lon", bit_number)
    partner_start = (lon_count - 1 - lax.axis_index("lon")) * breadth
    local_cols = fold_partner - partner_start
    folded = jnp.take(mirrored, local_cols, axis=1)
    at_top = lax.axis_index("lat") == lax.axis_size("lat") - 1
    above = jnp.where(at_top, folded, from_north)
    upper = jnp.concatenate([tokens[half_win:], above], axis=0)
    from_east = from_behind(upper[:, :half_win], "lon", -1)
    shifted = jnp.concatenate([upper[:, half_win:], from_east], axis=1)
    attended = run_windows(shifted, ocean_flags, in_weight, out_weight, norm_gain)
    quadrants = jnp.concatenate(
        [attended[0::2, 0::2], attended[1::2, 0::2], attended[0::2, 1::2], attended[1::2, 1::2]],
        axis=-1,
    )
    flat_quads = quadrants.reshape(-1, quadrants.shape[-1])
    merge_normed = layer_norm(flat_quads.astype(jnp.float32), merge_gain).astype(jnp.bfloat16)
    merged = jnp.dot(
        merge_normed,
        lax.all_gather(merge_weight, "lat", axis=0, tiled=True),
        preferred_element_type=jnp.float32,
    )
    return merged.astype(jnp.bfloat16).reshape(height // 2, breadth // 2, merge_weight.shape[1])


def solution(mesh):
    placed = (
        P("lat", "lon", None),
        P(),
        P("lat", None),
        P("lat", None),
        P(),
        P("lat", None),
        P("lat", "lon"),
        P("lon"),
    )
    return jax.shard_map(
        per_device, mesh=mesh, in_specs=placed, out_specs=P("lat", "lon", None), check_vma=False
    )
```

profile of v0, /device:TPU:0, one launch (start us, length us, event | category | flops | bytes accessed | tf_op | source)
XLA Modules:
  0.0 127.7 jit_solution(11649487323064791258)
XLA Ops:
  6.5 0.7 all-gather.3.cloned.1.call-update
  7.3 1.3 fusion.33
  8.8 0.3 rev.3
  9.2 3.1 %collective-permute-start = (bf16[8,32,768]{2,0,1:T(8,128)(2,1)S(1)}, bf16[8,32,768]{2,0,1:T(8,128)(2,1)S(1)}, u32[]{:S(2)}, u32[]{:S(2)}) collective-permute-start(bf16[8,32,768]{2,0,1:T(8,128)(2,1)S(1)} %rev.3), channel_id=1, source_target_pairs={{0,4},{4,0},{8,12},{12,8},{16,20},{20,16},{24,28},{28,24},{1,5},{5... | collective-permute-start | bytes 1179656 | tf_op jit(solution)/shard_map/ppermute | solution.py:23
  12.2 9.1 %collective-permute-done = bf16[8,32,768]{2,0,1:T(8,128)(2,1)S(1)} collective-permute-done((bf16[8,32,768]{2,0,1:T(8,128)(2,1)S(1)}, bf16[8,32,768]{2,0,1:T(8,128)(2,1)S(1)}, u32[]{:S(2)}, u32[]{:S(2)}) %collective-permute-start) | collective-permute-done | bytes 393248 | tf_op jit(solution)/shard_map/ppermute | solution.py:23
  21.4 1.8 %collective-permute-start.1 = (bf16[8,32,768]{2,0,1:T(8,128)(2,1)S(1)}, bf16[8,32,768]{2,0,1:T(8,128)(2,1)}, u32[]{:S(2)}, u32[]{:S(2)}) collective-permute-start(bf16[8,32,768]{2,0,1:T(8,128)(2,1)S(1)} %collective-permute-done), channel_id=1, source_target_pairs={{0,8},{4,12},{8,0},{12,4},{16,24},{20,28},{24,16},{28,20},{1,9},{5... | collective-permute-start | bytes 1179656 | tf_op jit(solution)/shard_map/ppermute | solution.py:23
  23.1 8.6 %collective-permute-done.1 = bf16[8,32,768]{2,0,1:T(8,128)(2,1)} collective-permute-done((bf16[8,32,768]{2,0,1:T(8,128)(2,1)S(1)}, bf16[8,32,768]{2,0,1:T(8,128)(2,1)}, u32[]{:S(2)}, u32[]{:S(2)}) %collective-permute-start.1) | collective-permute-done | bytes 393248 | tf_op jit(solution)/shard_map/ppermute | solution.py:23
  31.7 2.5 %collective-permute-start.2 = (bf16[8,32,768]{2,0,1:T(8,128)(2,1)}, bf16[8,32,768]{2,0,1:T(8,128)(2,1)}, u32[]{:S(2)}, u32[]{:S(2)}) collective-permute-start(bf16[8,32,768]{2,0,1:T(8,128)(2,1)} %collective-permute-done.1), channel_id=1, source_target_pairs={{0,16},{4,20},{8,24},{12,28},{16,0},{20,4},{24,8},{28,12},{1,17},{... | collective-permute-start | bytes 1179656 | tf_op jit(solution)/shard_map/ppermute | solution.py:23
  34.5 1.3 %collective-permute-start.3 = (bf16[8,32,768]{2,0,1:T(8,128)(2,1)S(1)}, bf16[8,32,768]{2,0,1:T(8,128)(2,1)S(1)}, u32[]{:S(2)}, u32[]{:S(2)}) collective-permute-start(bf16[8,32,768]{2,0,1:T(8,128)(2,1)S(1)} %copy.33), channel_id=1, source_target_pairs={{1,0},{2,1},{3,2},{5,4},{6,5},{7,6},{9,8},{10,9},{11,10},{13,12},{... | collective-permute-start | bytes 1179656 | tf_op jit(solution)/shard_map/ppermute | solution.py:17
  35.9 14.9 %collective-permute-done.2 = bf16[8,32,768]{2,0,1:T(8,128)(2,1)} collective-permute-done((bf16[8,32,768]{2,0,1:T(8,128)(2,1)}, bf16[8,32,768]{2,0,1:T(8,128)(2,1)}, u32[]{:S(2)}, u32[]{:S(2)}) %collective-permute-start.2) | collective-permute-done | bytes 393248 | tf_op jit(solution)/shard_map/ppermute | solution.py:23
  50.8 1.6 %gather_fusion = bf16[32,8,768]{2,1,0:T(8,128)(2,1)S(1)} fusion(bf16[8,32,768]{2,0,1:T(8,128)(2,1)} %collective-permute-done.2, s32[1024]{0:T(1024)S(1)} %pad_clamp_fusion), kind=kCustom, calls=%fused_computation | custom fusion | bytes 786560 | tf_op jit(solution)/shard_map/jit(_take)/gather | solution.py:112
  52.7 4.2 %collective-permute-start.4 = (bf16[32,8,768]{2,1,0:T(8,128)(2,1)S(1)}, bf16[32,8,768]{2,1,0:T(8,128)(2,1)S(1)}, u32[]{:S(2)}, u32[]{:S(2)}) collective-permute-start(bf16[32,8,768]{2,1,0:T(8,128)(2,1)S(1)} %pad_maximum_fusion.1), channel_id=1, source_target_pairs={{0,28},{4,0},{8,4},{12,8},{16,12},{20,16},{24,20},{28,24},{1,29},{... | collective-permute-start | bytes 1179656 | tf_op jit(solution)/shard_map/ppermute | solution.py:29
  56.9 7.6 %all_gather.10 = bf16[384,768]{1,0:T(8,128)(2,1)S(1)} all-gather(bf16[96,768]{1,0:T(8,128)(2,1)S(1)} %copy-done.1), channel_id=1, replica_groups=mesh['lon'=8,'lat'=4] {'lat'}, dimensions={0}, use_global_device_ids=true | all-gather | bytes 737280 | tf_op jit(solution)/shard_map/all_gather | solution.py:102
  64.6 0.8 collective-permute-done.4
  65.7 0.5 copy-done.4
  66.3 42.9 %while.10 = (s32[]{:T(128)}, bf16[4,256,768]{2,1,0:T(8,128)(2,1)}, bf16[4,256,768]{2,1,0:T(8,128)(2,1)S(1)}, s32[4]{0:T(128)S(1)}, f32[768]{0:T(1024)S(1)}, /*in...) while((s32[]{:T(128)}, bf16[4,256,768]{2,1,0:T(8,128)(2,1)}, ...), condition=%wide.region_5.6_spmd, body=%wide.region_0.5_spmd.sunk | while | flops 711918080 | bytes 14588030 | solution.py:83
  66.4 0.2 fusion.63
  66.6 2.3 %convolution_convert_fusion.3 = bf16[256,1152]{1,0:T(8,128)(2,1)S(1)} fusion(bf16[768,1152]{1,0:T(8,128)(2,1)} %get-tuple-element.142, f32[768]{0:T(1024)S(1)} %get-tuple-element.141, f32[256]{0:T(256)S(1)} %add_rsqrt_fusion.3, f32[256]{0:T(256)S(1)} %broadcast_multiply_fusion.3, bf16[4,256,768]{2,1,0:T(8,128)(2,1)S(1)} %get-tuple-element.139, ...), kind=kOutput, calls=%fused_computation.6.clone.1 | convolution fusion | flops 454262784 | bytes 2758660 | tf_op jit(solution)/shard_map/while/body/eval_jaxpr/dot_general | solution.py:55
  69.3 2.8 %fusion.65 = (f32[12,256]{1,0:T(8,128)S(1)}, f32[12,256,256]{1,2,0:T(8,128)}) fusion(bf16[256,12,32]{0,2,1:T(8,128)(2,1)S(1)} %bitcast.93, bf16[256,12,32]{0,2,1:T(8,128)(2,1)S(1)} %bitcast.94), kind=kOutput, calls=%fused_computation.52.clone.1 | convolution fusion | flops 52691200 | bytes 3551232 | tf_op jit(solution)/shard_map/while/body/eval_jaxpr/sub | solution.py:63
  72.3 2.3 %fusion.66 = bf16[12,32,256]{2,1,0:T(8,128)(2,1)S(1)} fusion(bf16[256,12,32]{0,2,1:T(8,128)(2,1)S(1)} %bitcast.95, f32[12,256,256]{1,2,0:T(8,128)} %get-tuple-element.117, f32[12,256]{1,0:T(8,128)S(1)} %get-tuple-element.118), kind=kOutput, calls=%fused_computation.14.clone.1 | convolution fusion | flops 52002816 | bytes 3551232 | tf_op jit(solution)/shard_map/while/body/eval_jaxpr/hqk,khd->qhd/dot_general | solution.py:65
  74.6 0.6 dynamic_slice.24
  75.8 1.2 fusion.67
  77.4 2.3 %convolution_convert_fusion.3 = bf16[256,1152]{1,0:T(8,128)(2,1)S(1)} fusion(bf16[768,1152]{1,0:T(8,128)(2,1)} %get-tuple-element.142, f32[768]{0:T(1024)S(1)} %get-tuple-element.141, f32[256]{0:T(256)S(1)} %add_rsqrt_fusion.3, f32[256]{0:T(256)S(1)} %broadcast_multiply_fusion.3, bf16[4,256,768]{2,1,0:T(8,128)(2,1)S(1)} %get-tuple-element.139, ...), kind=kOutput, calls=%fused_computation.6.clone.1 | convolution fusion | flops 454262784 | bytes 2758660 | tf_op jit(solution)/shard_map/while/body/eval_jaxpr/dot_general | solution.py:55
  80.0 2.8 %fusion.65 = (f32[12,256]{1,0:T(8,128)S(1)}, f32[12,256,256]{1,2,0:T(8,128)}) fusion(bf16[256,12,32]{0,2,1:T(8,128)(2,1)S(1)} %bitcast.93, bf16[256,12,32]{0,2,1:T(8,128)(2,1)S(1)} %bitcast.94), kind=kOutput, calls=%fused_computation.52.clone.1 | convolution fusion | flops 52691200 | bytes 3551232 | tf_op jit(solution)/shard_map/while/body/eval_jaxpr/sub | solution.py:63
  83.0 2.3 %fusion.66 = bf16[12,32,256]{2,1,0:T(8,128)(2,1)S(1)} fusion(bf16[256,12,32]{0,2,1:T(8,128)(2,1)S(1)} %bitcast.95, f32[12,256,256]{1,2,0:T(8,128)} %get-tuple-element.117, f32[12,256]{1,0:T(8,128)S(1)} %get-tuple-element.118), kind=kOutput, calls=%fused_computation.14.clone.1 | convolution fusion | flops 52002816 | bytes 3551232 | tf_op jit(solution)/shard_map/while/body/eval_jaxpr/hqk,khd->qhd/dot_general | solution.py:65
  85.3 0.6 dynamic_slice.24
  86.5 1.1 fusion.67
  88.1 2.3 %convolution_convert_fusion.3 = bf16[256,1152]{1,0:T(8,128)(2,1)S(1)} fusion(bf16[768,1152]{1,0:T(8,128)(2,1)} %get-tuple-element.142, f32[768]{0:T(1024)S(1)} %get-tuple-element.141, f32[256]{0:T(256)S(1)} %add_rsqrt_fusion.3, f32[256]{0:T(256)S(1)} %broadcast_multiply_fusion.3, bf16[4,256,768]{2,1,0:T(8,128)(2,1)S(1)} %get-tuple-element.139, ...), kind=kOutput, calls=%fused_computation.6.clone.1 | convolution fusion | flops 454262784 | bytes 2758660 | tf_op jit(solution)/shard_map/while/body/eval_jaxpr/dot_general | solution.py:55
  90.7 2.8 %fusion.65 = (f32[12,256]{1,0:T(8,128)S(1)}, f32[12,256,256]{1,2,0:T(8,128)}) fusion(bf16[256,12,32]{0,2,1:T(8,128)(2,1)S(1)} %bitcast.93, bf16[256,12,32]{0,2,1:T(8,128)(2,1)S(1)} %bitcast.94), kind=kOutput, calls=%fused_computation.52.clone.1 | convolution fusion | flops 52691200 | bytes 3551232 | tf_op jit(solution)/shard_map/while/body/eval_jaxpr/sub | solution.py:63
  93.7 2.3 %fusion.66 = bf16[12,32,256]{2,1,0:T(8,128)(2,1)S(1)} fusion(bf16[256,12,32]{0,2,1:T(8,128)(2,1)S(1)} %bitcast.95, f32[12,256,256]{1,2,0:T(8,128)} %get-tuple-element.117, f32[12,256]{1,0:T(8,128)S(1)} %get-tuple-element.118), kind=kOutput, calls=%fused_computation.14.clone.1 | convolution fusion | flops 52002816 | bytes 3551232 | tf_op jit(solution)/shard_map/while/body/eval_jaxpr/hqk,khd->qhd/dot_general | solution.py:65
  96.0 0.6 dynamic_slice.24
  97.3 1.2 fusion.67
  98.8 2.3 %convolution_convert_fusion.3 = bf16[256,1152]{1,0:T(8,128)(2,1)S(1)} fusion(bf16[768,1152]{1,0:T(8,128)(2,1)} %get-tuple-element.142, f32[768]{0:T(1024)S(1)} %get-tuple-element.141, f32[256]{0:T(256)S(1)} %add_rsqrt_fusion.3, f32[256]{0:T(256)S(1)} %broadcast_multiply_fusion.3, bf16[4,256,768]{2,1,0:T(8,128)(2,1)S(1)} %get-tuple-element.139, ...), kind=kOutput, calls=%fused_computation.6.clone.1 | convolution fusion | flops 454262784 | bytes 2758660 | tf_op jit(solution)/shard_map/while/body/eval_jaxpr/dot_general | solution.py:55
  101.5 2.8 %fusion.65 = (f32[12,256]{1,0:T(8,128)S(1)}, f32[12,256,256]{1,2,0:T(8,128)}) fusion(bf16[256,12,32]{0,2,1:T(8,128)(2,1)S(1)} %bitcast.93, bf16[256,12,32]{0,2,1:T(8,128)(2,1)S(1)} %bitcast.94), kind=kOutput, calls=%fused_computation.52.clone.1 | convolution fusion | flops 52691200 | bytes 3551232 | tf_op jit(solution)/shard_map/while/body/eval_jaxpr/sub | solution.py:63
  104.5 2.3 %fusion.66 = bf16[12,32,256]{2,1,0:T(8,128)(2,1)S(1)} fusion(bf16[256,12,32]{0,2,1:T(8,128)(2,1)S(1)} %bitcast.95, f32[12,256,256]{1,2,0:T(8,128)} %get-tuple-element.117, f32[12,256]{1,0:T(8,128)S(1)} %get-tuple-element.118), kind=kOutput, calls=%fused_computation.14.clone.1 | convolution fusion | flops 52002816 | bytes 3551232 | tf_op jit(solution)/shard_map/while/body/eval_jaxpr/hqk,khd->qhd/dot_general | solution.py:65
  106.7 0.6 dynamic_slice.24
  108.0 1.2 fusion.67
  109.2 1.6 %copy.30 = bf16[2,16,2,16,768]{4,3,2,1,0:T(8,128)(2,1)S(1)} copy(bf16[2,16,2,16,768]{4,3,1,2,0:T(8,128)(2,1)} %bitcast.13) | data formatting | bytes 3145728 | tf_op jit(solution)/shard_map/transpose | solution.py:48
  110.8 0.7 slice.41
  111.5 0.9 slice.42
  112.4 0.7 slice.43
  113.0 0.9 slice.44
  113.9 0.3 fusion.30
  114.3 0.5 multiply_reduce_fusion.1
  115.0 0.4 maximum_convert_fusion
  115.3 0.3 copy-done.2
  115.7 0.7 fusion.28
  116.4 4.5 %convolution_convert_fusion.1 = bf16[256,768]{1,0:T(8,128)(2,1)} fusion(bf16[256,3072]{1,0:T(8,128)(2,1)S(1)} %fusion.28, bf16[3072,768]{1,0:T(8,128)(2,1)} %all-gather.5.cloned.1.call-done), kind=kOutput, calls=%fused_computation.41 | convolution fusion | flops 1208156160 | bytes 6684672 | tf_op jit(solution)/shard_map/dot_general | solution.py:125
  (64 shorter events, 4.9 us)
Async XLA Ops:
  6.5 59.2 %all-gather.3.cloned.1.call-start = ((), (), s32[]{:S(2)}) async-start(), calls=%async_computation | async-start | bytes 2211840 | tf_op jit(solution)/shard_map/all_gather | solution.py:101
  7.3 28.5 %copy-start = (bf16[32,32,768]{2,1,0:T(8,128)(2,1)S(1)}, bf16[32,32,768]{2,1,0:T(8,128)(2,1)}, u32[]{:S(2)}) copy-start(bf16[32,32,768]{2,1,0:T(8,128)(2,1)} %param.10) | copy-start | bytes 4718596
  7.3 109.1 %all-gather.5.cloned.1.call-start = ((), (), s32[]{:S(2)}) async-start(), calls=%async_computation.1 | async-start | bytes 5898240 | tf_op jit(solution)/shard_map/all_gather | solution.py:127
  9.2 26.7 %copy-start.3 = (s32[32]{0:T(128)S(1)}, s32[32]{0:T(128)}, u32[]{:S(2)}) copy-start(s32[32]{0:T(128)} %param.17) | copy-start | bytes 388
  9.2 12.2 %collective-permute-start = (bf16[8,32,768]{2,0,1:T(8,128)(2,1)S(1)}, bf16[8,32,768]{2,0,1:T(8,128)(2,1)S(1)}, u32[]{:S(2)}, u32[]{:S(2)}) collective-permute-start(bf16[8,32,768]{2,0,1:T(8,128)(2,1)S(1)} %rev.3), channel_id=1, source_target_pairs={{0,4},{4,0},{8,12},{12,8},{16,20},{20,16},{24,28},{28,24},{1,5},{5... | collective-permute-start | bytes 1179656 | tf_op jit(solution)/shard_map/ppermute | solution.py:23
  21.4 10.4 %collective-permute-start.1 = (bf16[8,32,768]{2,0,1:T(8,128)(2,1)S(1)}, bf16[8,32,768]{2,0,1:T(8,128)(2,1)}, u32[]{:S(2)}, u32[]{:S(2)}) collective-permute-start(bf16[8,32,768]{2,0,1:T(8,128)(2,1)S(1)} %collective-permute-done), channel_id=1, source_target_pairs={{0,8},{4,12},{8,0},{12,4},{16,24},{20,28},{24,16},{28,20},{1,9},{5... | collective-permute-start | bytes 1179656 | tf_op jit(solution)/shard_map/ppermute | solution.py:23
  31.7 19.1 %collective-permute-start.2 = (bf16[8,32,768]{2,0,1:T(8,128)(2,1)}, bf16[8,32,768]{2,0,1:T(8,128)(2,1)}, u32[]{:S(2)}, u32[]{:S(2)}) collective-permute-start(bf16[8,32,768]{2,0,1:T(8,128)(2,1)} %collective-permute-done.1), channel_id=1, source_target_pairs={{0,16},{4,20},{8,24},{12,28},{16,0},{20,4},{24,8},{28,12},{1,17},{... | collective-permute-start | bytes 1179656 | tf_op jit(solution)/shard_map/ppermute | solution.py:23
  34.5 17.9 %collective-permute-start.3 = (bf16[8,32,768]{2,0,1:T(8,128)(2,1)S(1)}, bf16[8,32,768]{2,0,1:T(8,128)(2,1)S(1)}, u32[]{:S(2)}, u32[]{:S(2)}) collective-permute-start(bf16[8,32,768]{2,0,1:T(8,128)(2,1)S(1)} %copy.33), channel_id=1, source_target_pairs={{1,0},{2,1},{3,2},{5,4},{6,5},{7,6},{9,8},{10,9},{11,10},{13,12},{... | collective-permute-start | bytes 1179656 | tf_op jit(solution)/shard_map/ppermute | solution.py:17
  52.6 4.3 %copy-start.5 = (s32[2,2]{1,0:T(2,128)S(1)}, s32[2,2]{1,0:T(2,128)}, u32[]{:S(2)}) copy-start(s32[2,2]{1,0:T(2,128)} %param.16) | copy-start | bytes 52
  52.6 4.3 %copy-start.1 = (bf16[96,768]{1,0:T(8,128)(2,1)S(1)}, bf16[96,768]{1,0:T(8,128)(2,1)}, u32[]{:S(2)}) copy-start(bf16[96,768]{1,0:T(8,128)(2,1)} %param.13) | copy-start | bytes 442372
  52.7 12.7 %collective-permute-start.4 = (bf16[32,8,768]{2,1,0:T(8,128)(2,1)S(1)}, bf16[32,8,768]{2,1,0:T(8,128)(2,1)S(1)}, u32[]{:S(2)}, u32[]{:S(2)}) collective-permute-start(bf16[32,8,768]{2,1,0:T(8,128)(2,1)S(1)} %pad_maximum_fusion.1), channel_id=1, source_target_pairs={{0,28},{4,0},{8,4},{12,8},{16,12},{20,16},{24,20},{28,24},{1,29},{... | collective-permute-start | bytes 1179656 | tf_op jit(solution)/shard_map/ppermute | solution.py:29
  65.6 0.7 copy-start.4
  115.0 0.7 copy-start.2
Sparse Core Ops, SparseCore 0:
  8.9 23.4 all-gather.2
  57.0 34.6 all-gather.4
where the time goes:
time: 128 us
  matrix products  38.7 us (30%)
  waiting for transfers between devices  34.1 us (27%)
  local copies, waits for them, and re-layouts  14.2 us (11%)
  between operations  13.7 us (11%)
  starting transfers between devices  12.9 us (10%)
  blocking collectives  7.55 us (6%)
  other arithmetic  3.89 us (3%)
  loops' own time  2.7 us (2%)
    ppermute x3, waiting for transfers between devices, partner(): return lax.ppermute(value, axis, pairs)  32.6 us
    sub x4, matrix products, window_branch(): lifted = jnp.exp(scores - highest)  11.4 us
    dot_general x4, matrix products, window_branch(): jnp.einsum('hqk,khd->qhd', weights, value_cols, preferred_element_type=jn...  9.11 us
    dot_general x4, matrix products, window_branch(): jnp.dot(normed, in_weight, preferred_element_type=jnp.float32)  9.09 us
    all_gather x1, blocking collectives, per_device(): lax.all_gather(outproj_weight, 'lat', axis=0, tiled=True)  7.55 us
    ppermute x3, starting transfers between devices, partner(): return lax.ppermute(value, axis, pairs)  7.39 us
    dot_general x4, matrix products, window_branch(): return jnp.dot(mixed_heads, out_weight, preferred_element_type=jnp.float32)  4.63 us
    dot_general x1, matrix products, per_device(): jnp.dot(merge_normed, lax.all_gather(merge_weight, 'lat', axis=0, tiled=T...  4.46 us
  transfers between devices with their start and end apart: 7, of which 4 were waited for; matrix products, arithmetic and copies ran while one was open for 40% of the time, Pallas kernels for 0%

commit v1 on v0

v1 whole, which is shorter than its diff:
```python
import functools
import math

import jax
import jax.numpy as jnp
from jax import lax
from jax.experimental import pallas as pl
from jax.experimental.pallas import tpu as pltpu
from jax.sharding import PartitionSpec as P

HEADS = 12
HD = 32
WIN = 16
HALF = WIN // 2
GROUP = 4
epsilon = 1e-05

MESH = pl.DeviceIdType.MESH


def kernel(
    spread,
    tokens,
    norm_gain,
    in_shard,
    out_shard,
    merge_gain,
    merge_shard,
    flags,
    partners,
    out,
    windows,
    mirror,
    corner,
    order,
    w_in,
    w_out,
    w_merge,
    packed_ref,
    mixed_ref,
    merge_in,
    local_sem,
    halo_send,
    halo_recv,
    w_local,
    w_send,
    w_recv,
):
    lat, lon = lax.axis_index("lat"), lax.axis_index("lon")
    n_lat, n_lon = lax.axis_size("lat"), lax.axis_size("lon")
    rows, width = tokens.shape[0], tokens.shape[3]
    head_width = HEADS * HD
    is_top = lat == n_lat - 1
    west, east = lax.rem(lon + n_lon - 1, n_lon), lax.rem(lon + 1, n_lon)
    south, north = lax.rem(lat + n_lat - 1, n_lat), lax.rem(lat + 1, n_lat)
    facing = n_lon - 1 - lon
    mate = lat + 1 - 2 * lax.rem(lat, 2)
    across = lax.rem(lat + 2, 4)
    across_mate = mate + across - lat
    side = lax.rem(lon, 2)
    beside = lon + 1 - 2 * side

    local = []

    def move(src, dst):
        copy = pltpu.make_async_copy(src, dst, local_sem.at[len(local)])
        copy.start()
        local.append(copy)

    move(tokens.at[pl.ds(HALF, WIN), 1], windows.at[0, 0])
    move(tokens.at[pl.ds(HALF, WIN), 2], windows.at[0, 1])
    move(tokens.at[pl.ds(HALF, WIN), 3], windows.at[1, 0])
    tail = rows - HALF
    for at, (w, h) in ((1, (2, 0)), (2, (2, 1)), (3, (3, 0))):
        move(tokens.at[pl.ds(tail, HALF), at], windows.at[w, h, pl.ds(0, HALF)])

    n_in, n_out, n_merge = in_shard.shape[0], out_shard.shape[0], merge_shard.shape[0]
    half_merge = n_merge // 2 if spread else n_merge
    items = [(in_shard, 0, n_in, w_in), (out_shard, 0, n_out, w_out), (merge_shard, 0, half_merge, w_merge)]
    if spread:
        items.append((merge_shard, half_merge, half_merge, w_merge))
    size_of = [n_in, n_out, n_merge, n_merge]

    def place(k, shard, first, count):
        _, row0, _, dst = items[k]
        start = shard * size_of[k] + row0 + first
        return dst.at[pl.ds(pl.multiple_of(start, 16), count), :]

    own = []
    for k, (src, row0, count, _) in enumerate(items):
        me = lat if spread else 0
        copy = pltpu.make_async_copy(src.at[pl.ds(row0, count), :], place(k, me, 0, count), w_local.at[k])
        copy.start()
        own.append(copy)

    peers = [
        (south, lon), (north, lon), (lat, west), (lat, east), (south, west), (north, east), (lat, facing),
    ]
    if spread:
        peers += [(mate, lon), (across, lon), (lat, beside)]
    barrier = pltpu.get_barrier_semaphore()
    for a, b in peers:
        pl.semaphore_signal(barrier, inc=1, device_id={"lat": a, "lon": b}, device_id_type=MESH)

    t = lax.broadcasted_iota(jnp.int32, order.shape, 0)
    s = lax.broadcasted_iota(jnp.int32, order.shape, 1)
    quad, i, j = t >> 6, (t >> 3) & 7, t & 7
    r, c = 2 * i + (quad & 1), 2 * j + (quad >> 1)
    order[...] = jnp.where(s == (c >> 3) * 128 + r * 8 + (c & 7), 1.0, 0.0).astype(jnp.bfloat16)

    pl.semaphore_wait(barrier, len(peers))

    def remote(src, dst, send, recv, a, b):
        return pltpu.make_async_remote_copy(
            src_ref=src, dst_ref=dst, send_sem=send, recv_sem=recv,
            device_id={"lat": a, "lon": b}, device_id_type=MESH,
        )

    def hop(k, step):
        _, row0, count, _ = items[k]
        half = count // 2
        near, far = side * half, (1 - side) * half
        send, recv = w_send.at[k, step], w_recv.at[k, step]
        src = items[k][0]
        if step == 0:
            return remote(src.at[pl.ds(row0, count), :], place(k, lat, 0, count), send, recv, mate, lon)
        if step == 1:
            first = pl.multiple_of(row0 + near, 16)
            return remote(src.at[pl.ds(first, half), :], place(k, lat, near, half), send, recv, across, lon)
        if step == 2:
            ref = place(k, across, near, half)
            return remote(ref, ref, send, recv, lat, beside)
        if step == 3:
            ref = place(k, across, near, half)
            return remote(ref, ref, send, recv, mate, lon)
        ref = place(k, across, far, half)
        return remote(ref, ref, send, recv, mate, lon)

    def halo(n):
        head = pl.ds(0, HALF)
        late = pl.ds(HALF, HALF)
        if n < 3:
            w, h = ((2, 0), (2, 1), (3, 0))[n]
            return remote(tokens.at[head, n + 1], windows.at[w, h, late], halo_send.at[n], halo_recv.at[n], south, lon)
        if n == 3:
            return remote(tokens.at[head, 0], windows.at[3, 1, late], halo_send.at[3], halo_recv.at[3], south, west)
        if n == 4:
            return remote(tokens.at[pl.ds(HALF, WIN), 0], windows.at[1, 1], halo_send.at[4], halo_recv.at[4], lat, west)
        if n == 5:
            return remote(tokens.at[pl.ds(tail, HALF), 0], windows.at[3, 1, head], halo_send.at[5], halo_recv.at[5], lat, west)
        if n == 6:
            return remote(tokens.at[pl.ds(tail, HALF)], mirror, halo_send.at[6], halo_recv.at[6], lat, facing)
        return remote(corner, windows.at[3, 1, late], halo_send.at[7], halo_recv.at[7], lat, west)

    if spread:
        hop(0, 1).start()
        hop(0, 0).start()
        hop(1, 1).start()
        hop(1, 0).start()
    halo(4).start()

    @pl.when(is_top)
    def _():
        halo(6).start()

    @pl.when(lat > 0)
    def _():
        for n in range(4):
            halo(n).start()

    halo(5).start()
    if spread:
        for k in (2, 3):
            hop(k, 1).start()
            hop(k, 0).start()

        def pass_on(k):
            hop(k, 1).wait_recv()
            hop(k, 2).start()
            hop(k, 3).start()

        def pass_far(k):
            hop(k, 2).wait_recv()
            hop(k, 4).start()

        def arrived(k):
            for step in (0, 3, 4):
                hop(k, step).wait_recv()

        pass_on(0)
        pass_on(1)
        pass_far(0)
        pass_far(1)
        own[0].wait()
        own[1].wait()
        arrived(0)
        arrived(1)
    else:
        own[0].wait()
        own[1].wait()

    lane = lax.broadcasted_iota(jnp.int32, (1, GROUP * HD), 1)
    ones = jnp.ones((WIN * WIN, GROUP * HD), jnp.bfloat16)

    def fold():
        halo(6).wait_recv()
        tt = lax.broadcasted_iota(jnp.int32, (WIN * WIN, WIN * WIN), 0)
        ss = lax.broadcasted_iota(jnp.int32, (WIN * WIN, WIN * WIN), 1)
        column = (tt >> 6) * HALF + (tt & 7)
        first = (n_lon - 1 - lon) * (4 * HALF)
        source = jnp.zeros_like(tt)
        for k in range(4 * HALF):
            source = jnp.where(column == k, partners[k] - first, source)
        source = source + (HALF - 1 - ((tt >> 3) & 7)) * (4 * HALF)
        pick = jnp.where(ss == source, 1.0, 0.0).astype(jnp.bfloat16)
        raw = mirror[...].astype(jnp.float32).reshape(WIN * WIN, width).astype(jnp.bfloat16)
        folded = jnp.dot(pick, raw, preferred_element_type=jnp.float32)
        part = folded.reshape(4, HALF, HALF, width).astype(jnp.bfloat16)
        corner[...] = part[0]
        windows[2, 0, pl.ds(HALF, HALF)] = part[1]
        windows[2, 1, pl.ds(HALF, HALF)] = part[2]
        windows[3, 0, pl.ds(HALF, HALF)] = part[3]
        halo(7).start()

    def body(w, carry):
        @pl.when(w == 0)
        def _():
            local[0].wait()
            local[1].wait()

        @pl.when(w == 1)
        def _():
            if spread:
                pass_on(2)
            local[2].wait()
            halo(4).wait_recv()

        @pl.when(w == 2)
        def _():
            if spread:
                pass_on(3)
                pass_far(2)
            local[3].wait()
            local[4].wait()

            @pl.when(is_top)
            def _():
                fold()

            @pl.when(lat < n_lat - 1)
            def _():
                halo(0).wait_recv()
                halo(1).wait_recv()

        @pl.when(w == 3)
        def _():
            if spread:
                pass_far(3)
            local[5].wait()
            halo(5).wait_recv()

            @pl.when(is_top)
            def _():
                halo(7).wait_recv()

            @pl.when(lat < n_lat - 1)
            def _():
                halo(2).wait_recv()
                halo(3).wait_recv()

        raw = windows[w].astype(jnp.float32).reshape(WIN * WIN, width).astype(jnp.bfloat16)
        x = jnp.dot(order[...], raw, preferred_element_type=jnp.float32)
        center = x - jnp.sum(x, axis=-1, keepdims=True) * (1.0 / width)
        spread_of = jnp.sum(center * center, axis=-1, keepdims=True) * (1.0 / width)
        normed = (center * lax.rsqrt(spread_of + epsilon) * norm_gain[...]).astype(jnp.bfloat16)
        packed = jnp.dot(normed, w_in[...], preferred_element_type=jnp.float32)
        factor = HD ** (-0.5) * math.log2(math.e)
        packed_ref[:, :head_width] = (packed[:, :head_width] * factor).astype(jnp.bfloat16)
        packed_ref[:, head_width:] = packed[:, head_width:].astype(jnp.bfloat16)
        for g in range(HEADS // GROUP):
            at = g * GROUP * HD
            q = packed_ref[:, at : at + GROUP * HD]
            k = packed_ref[:, head_width + at : head_width + at + GROUP * HD]
            v = packed_ref[:, 2 * head_width + at : 2 * head_width + at + GROUP * HD]
            v = jnp.concatenate([v, ones], axis=1)
            mixed = jnp.zeros((WIN * WIN, GROUP * HD), jnp.float32)
            for h in range(GROUP):
                mine = (lane >= h * HD) & (lane < (h + 1) * HD)
                q_own = jnp.where(mine, q.astype(jnp.float32), 0.0).astype(jnp.bfloat16)
                scores = lax.dot_general(
                    q_own, k, (((1,), (1,)), ((), ())), preferred_element_type=jnp.float32
                )
                highest = jnp.max(scores, axis=-1, keepdims=True)
                lifted = jnp.exp2(scores - highest).astype(jnp.bfloat16)
                both = jnp.dot(lifted, v, preferred_element_type=jnp.float32)
                share = both[:, : GROUP * HD] / both[:, GROUP * HD :]
                mixed = jnp.where(mine, share, mixed)
            mixed_ref[:, at : at + GROUP * HD] = mixed.astype(jnp.bfloat16)
        branch = jnp.dot(mixed_ref[...], w_out[...], preferred_element_type=jnp.float32)
        kept = jnp.where(flags[w // 2, lax.rem(w, 2)] > 0, branch, 0.0)
        attended = (x + kept).astype(jnp.bfloat16).astype(jnp.float32)
        count = WIN * WIN // 4
        quads = [attended[n * count : (n + 1) * count] for n in range(4)]
        total = sum(jnp.sum(quad, axis=-1, keepdims=True) for quad in quads)
        mean = total * (1.0 / (4 * width))
        quads = [quad - mean for quad in quads]
        square = sum(jnp.sum(quad * quad, axis=-1, keepdims=True) for quad in quads)
        inverse = lax.rsqrt(square * (1.0 / (4 * width)) + epsilon)
        for n, quad in enumerate(quads):
            value = quad * inverse * merge_gain[n]
            merge_in[n, pl.ds(pl.multiple_of(w * count, count), count), :] = value.astype(jnp.bfloat16)
        return carry

    lax.fori_loop(0, 4, body, 0)

    def product(shard):
        weight = w_merge[pl.ds(pl.multiple_of(shard * width, width), width), :]
        return jnp.dot(merge_in[shard], weight, preferred_element_type=jnp.float32)

    if spread:
        own[2].wait()
        own[3].wait()
        total = product(lat)
        hop(2, 0).wait_recv()
        hop(3, 0).wait_recv()
        total = total + product(mate)
        total = total + product(across)
        for k in (2, 3):
            hop(k, 3).wait_recv()
            hop(k, 4).wait_recv()
        total = total + product(across_mate)
    else:
        own[2].wait()
        total = sum(product(n) for n in range(4))
    count = WIN * WIN // 4
    for w in range(4):
        piece = total[w * count : (w + 1) * count].reshape(HALF, HALF, total.shape[1])
        out[w // 2, :, w % 2] = piece.astype(out.dtype)

    if spread:
        for k in range(4):
            for step in range(5):
                hop(k, step).wait_send()
    halo(4).wait_send()
    halo(5).wait_send()

    @pl.when(is_top)
    def _():
        halo(6).wait_send()
        halo(7).wait_send()

    @pl.when(lat > 0)
    def _():
        for n in range(4):
            halo(n).wait_send()


def per_device(
    tokens, norm_gain, inproj_weight, outproj_weight, merge_gain, merge_weight, ocean_flags, fold_partner
):
    height, breadth, width = tokens.shape
    n_lat = lax.axis_size("lat")
    spread = (
        n_lat == 4
        and merge_weight.shape[0] == width
        and all(w.shape[0] % 32 == 0 for w in (inproj_weight, outproj_weight))
    )
    if not spread:
        inproj_weight, outproj_weight, merge_weight = (
            lax.all_gather(w, "lat", axis=0, tiled=True) for w in (inproj_weight, outproj_weight, merge_weight)
        )
    tall = n_lat if spread else 1
    in_rows, packed_width = inproj_weight.shape[0] * tall, inproj_weight.shape[1]
    out_rows = outproj_weight.shape[0] * tall
    merge_rows, merge_width = merge_weight.shape[0] * tall, merge_weight.shape[1]
    square = WIN * WIN
    vmem = pl.BlockSpec(memory_space=pltpu.VMEM)
    smem = pl.BlockSpec(memory_space=pltpu.SMEM)
    hbm = pl.BlockSpec(memory_space=pl.ANY)
    bf16 = jnp.bfloat16
    merged = pl.pallas_call(
        functools.partial(kernel, spread),
        out_shape=jax.ShapeDtypeStruct((2, HALF, 2, HALF, merge_width), bf16),
        in_specs=[hbm, vmem, hbm, hbm, vmem, hbm, smem, smem],
        out_specs=vmem,
        scratch_shapes=[
            pltpu.VMEM((4, 2, WIN, HALF, width), bf16),
            pltpu.VMEM((HALF, 4, HALF, width), bf16),
            pltpu.VMEM((HALF, HALF, width), bf16),
            pltpu.VMEM((square, square), bf16),
            pltpu.VMEM((in_rows, packed_width), bf16),
            pltpu.VMEM((out_rows, width), bf16),
            pltpu.VMEM((merge_rows, merge_width), bf16),
            pltpu.VMEM((square, packed_width), bf16),
            pltpu.VMEM((square, out_rows), bf16),
            pltpu.VMEM((4, square, width), bf16),
            pltpu.SemaphoreType.DMA((6,)),
            pltpu.SemaphoreType.DMA((8,)),
            pltpu.SemaphoreType.DMA((8,)),
            pltpu.SemaphoreType.DMA((4,)),
            pltpu.SemaphoreType.DMA((4, 5)),
            pltpu.SemaphoreType.DMA((4, 5)),
        ],
        compiler_params=pltpu.CompilerParams(
            collective_id=0, has_side_effects=True, vmem_limit_bytes=48 * 1024 * 1024
        ),
        name="window_attention_merge",
    )(
        tokens.reshape(height, breadth // HALF, HALF, width),
        norm_gain.reshape(1, width),
        inproj_weight,
        outproj_weight,
        merge_gain.reshape(4, 1, width),
        merge_weight,
        ocean_flags,
        fold_partner,
    )
    return merged.reshape(height // 2, breadth // 2, merge_width)


def solution(mesh):
    placed = (
        P("lat", "lon", None),
        P(),
        P("lat", None),
        P("lat", None),
        P(),
        P("lat", None),
        P("lat", "lon"),
        P("lon"),
    )
    return jax.shard_map(
        per_device, mesh=mesh, in_specs=placed, out_specs=P("lat", "lon", None), check_vma=False
    )
```

time: 128 us -> 58.8 us (0.46)
  the two profiles are of different devices: /device:TPU:0 before, /device:TPU:27 now
where the time goes in v1:
time: 58.8 us; the launch traced here: 58.5 us
  Pallas kernels  50.4 us (86%)
  local copies, waits for them, and re-layouts  8.08 us (14%)
    pallas_call x1, Pallas kernels, per_device(): pl.pallas_call(functools.partial(kernel, spread), out_shape=jax.ShapeDtyp...  50.4 us
    unnamed x15, local copies, waits for them, and re-layouts  7.39 us

profile of v1, /device:TPU:27, one launch (start us, length us, event | category | flops | bytes accessed | tf_op | source)
XLA Modules:
  0.0 58.5 jit_solution(15154198554515203605)
XLA Ops:
  0.0 0.7 %reshape.13.norm_gain = f32[1,768]{1,0:T(1,128)S(1)} reshape(f32[768]{0:T(1024)} %param.9) | data formatting | bytes 6144 | tf_op jit(solution)/shard_map/reshape | solution.py:410
  0.7 0.0 copy-start
  0.7 1.4 %copy-done = bf16[32,32,768]{2,1,0:T(8,128)(2,1)S(1)} copy-done((bf16[32,32,768]{2,1,0:T(8,128)(2,1)S(1)}, bf16[32,32,768]{2,1,0:T(8,128)(2,1)}, u32[]{:S(2)}) %copy-start) | copy-done | bytes 1572888
  2.1 0.0 copy-start.1
  2.1 1.3 %copy-done.1 = bf16[768,768]{1,0:T(8,128)(2,1)S(1)} copy-done((bf16[768,768]{1,0:T(8,128)(2,1)S(1)}, bf16[768,768]{1,0:T(8,128)(2,1)}, u32[]{:S(2)}) %copy-start.1) | copy-done | bytes 1179672
  3.4 0.0 copy-start.2
  3.4 1.0 %copy-done.2 = bf16[192,1152]{1,0:T(8,128)(2,1)S(1)} copy-done((bf16[192,1152]{1,0:T(8,128)(2,1)S(1)}, bf16[192,1152]{1,0:T(8,128)(2,1)}, u32[]{:S(2)}) %copy-start.2) | copy-done | bytes 442392
  4.4 0.0 copy-start.3
  4.4 0.9 %copy-done.3 = bf16[96,768]{1,0:T(8,128)(2,1)S(1)} copy-done((bf16[96,768]{1,0:T(8,128)(2,1)S(1)}, bf16[96,768]{1,0:T(8,128)(2,1)}, u32[]{:S(2)}) %copy-start.3) | copy-done | bytes 147480
  5.3 0.0 copy-start.4
  5.3 0.7 %copy-done.4 = f32[3072]{0:T(1024)S(1)} copy-done((f32[3072]{0:T(1024)S(1)}, f32[3072]{0:T(1024)}, u32[]{:S(2)}) %copy-start.4) | copy-done | bytes 12312
  6.0 0.0 copy-start.5
  6.0 0.7 %copy-done.5 = s32[2,2]{1,0:T(2,128)S(1)} copy-done((s32[2,2]{1,0:T(2,128)S(1)}, s32[2,2]{1,0:T(2,128)}, u32[]{:S(2)}) %copy-start.5) | copy-done | bytes 40
  6.7 0.0 copy-start.6
  6.7 0.7 %copy-done.6 = s32[32]{0:T(128)S(1)} copy-done((s32[32]{0:T(128)S(1)}, s32[32]{0:T(128)}, u32[]{:S(2)}) %copy-start.6) | copy-done | bytes 152
  7.3 50.4 %window_attention_merge.1 = bf16[2,8,2,8,768]{4,3,2,1,0:T(8,128)(2,1)S(1)} custom-call(bf16[32,4,8,768]{3,2,1,0:T(8,128)(2,1)S(1)} %bitcast.3, f32[1,768]{1,0:T(1,128)S(1)} %reshape.13.norm_gain, bf16[192,1152]{1,0:T(8,128)(2,1)S(1)} %copy-done.2, bf16[96,768]{1,0:T(8,128)(2,1)S(1)} %copy-done.3, f32[4,1,768]{2,1,0:T(1,128)S(1)} %bitcast.5, ...), custom_call_target="tpu_custom_call" | custom-call | tf_op jit(solution)/shard_map/window_attention_merge/pallas_call | solution.py:381
  57.7 0.7 %copy.10 = bf16[16,16,768]{2,1,0:T(8,128)(2,1)} copy(bf16[16,16,768]{2,1,0:T(8,128)(2,1)S(1)} %bitcast.4) | data formatting | bytes 786432
Async XLA Ops:
  0.7 1.4 %copy-start = (bf16[32,32,768]{2,1,0:T(8,128)(2,1)S(1)}, bf16[32,32,768]{2,1,0:T(8,128)(2,1)}, u32[]{:S(2)}) copy-start(bf16[32,32,768]{2,1,0:T(8,128)(2,1)} %param.8) | copy-start | bytes 4718596
  2.1 1.3 %copy-start.1 = (bf16[768,768]{1,0:T(8,128)(2,1)S(1)}, bf16[768,768]{1,0:T(8,128)(2,1)}, u32[]{:S(2)}) copy-start(bf16[768,768]{1,0:T(8,128)(2,1)} %merge_shard.1) | copy-start | bytes 3538948
  3.4 1.0 %copy-start.2 = (bf16[192,1152]{1,0:T(8,128)(2,1)S(1)}, bf16[192,1152]{1,0:T(8,128)(2,1)}, u32[]{:S(2)}) copy-start(bf16[192,1152]{1,0:T(8,128)(2,1)} %in_shard.1) | copy-start | bytes 1327108
  4.4 0.9 %copy-start.3 = (bf16[96,768]{1,0:T(8,128)(2,1)S(1)}, bf16[96,768]{1,0:T(8,128)(2,1)}, u32[]{:S(2)}) copy-start(bf16[96,768]{1,0:T(8,128)(2,1)} %out_shard.1) | copy-start | bytes 442372
  5.3 0.7 %copy-start.4 = (f32[3072]{0:T(1024)S(1)}, f32[3072]{0:T(1024)}, u32[]{:S(2)}) copy-start(f32[3072]{0:T(1024)} %param.12) | copy-start | bytes 36868
  6.0 0.7 %copy-start.5 = (s32[2,2]{1,0:T(2,128)S(1)}, s32[2,2]{1,0:T(2,128)}, u32[]{:S(2)}) copy-start(s32[2,2]{1,0:T(2,128)} %flags.1) | copy-start | bytes 52
  6.7 0.7 %copy-start.6 = (s32[32]{0:T(128)S(1)}, s32[32]{0:T(128)}, u32[]{:S(2)}) copy-start(s32[32]{0:T(128)} %partners.1) | copy-start | bytes 388

commit v2 on v1

--- a/solution.py
+++ b/solution.py
@@ -12,6 +12,7 @@
 HD = 32
 WIN = 16
 HALF = WIN // 2
+CHUNKS = 4
 GROUP = 4
 epsilon = 1e-05
 
@@ -57,8 +58,10 @@
     mate = lat + 1 - 2 * lax.rem(lat, 2)
     across = lax.rem(lat + 2, 4)
     across_mate = mate + across - lat
-    side = lax.rem(lon, 2)
-    beside = lon + 1 - 2 * side
+    odd, odd_pair = lax.rem(lon, 2), lax.rem(lon // 2, 2)
+    side = lax.rem(odd + odd_pair, 2)
+    beside = lon + 1 - 2 * odd
+    behind = lon + 2 - 4 * odd_pair
 
     local = []
 
@@ -75,11 +78,12 @@
         move(tokens.at[pl.ds(tail, HALF), at], windows.at[w, h, pl.ds(0, HALF)])
 
     n_in, n_out, n_merge = in_shard.shape[0], out_shard.shape[0], merge_shard.shape[0]
-    half_merge = n_merge // 2 if spread else n_merge
-    items = [(in_shard, 0, n_in, w_in), (out_shard, 0, n_out, w_out), (merge_shard, 0, half_merge, w_merge)]
-    if spread:
-        items.append((merge_shard, half_merge, half_merge, w_merge))
-    size_of = [n_in, n_out, n_merge, n_merge]
+    chunks = CHUNKS if spread else 1
+    items = [(in_shard, 0, n_in, w_in), (out_shard, 0, n_out, w_out)]
+    for n in range(chunks):
+        items.append((merge_shard, n * (n_merge // chunks), n_merge // chunks, w_merge))
+    size_of = [n_in, n_out] + [n_merge] * chunks
+    merge_items = range(2, 2 + chunks)
 
     def place(k, shard, first, count):
         _, row0, _, dst = items[k]
@@ -97,7 +101,7 @@
         (south, lon), (north, lon), (lat, west), (lat, east), (south, west), (north, east), (lat, facing),
     ]
     if spread:
-        peers += [(mate, lon), (across, lon), (lat, beside)]
+        peers += [(mate, lon), (across, lon), (lat, beside), (lat, behind)]
     barrier = pltpu.get_barrier_semaphore()
     for a, b in peers:
         pl.semaphore_signal(barrier, inc=1, device_id={"lat": a, "lon": b}, device_id_type=MESH)
@@ -127,13 +131,19 @@
         if step == 1:
             first = pl.multiple_of(row0 + near, 16)
             return remote(src.at[pl.ds(first, half), :], place(k, lat, near, half), send, recv, across, lon)
+        part = -(-half // 32) * 16
         if step == 2:
-            ref = place(k, across, near, half)
+            ref = place(k, across, near, part)
             return remote(ref, ref, send, recv, lat, beside)
         if step == 3:
+            ref = place(k, across, near + part, half - part)
+            return remote(ref, ref, send, recv, lat, behind)
+        if step == 4:
             ref = place(k, across, near, half)
-            return remote(ref, ref, send, recv, mate, lon)
-        ref = place(k, across, far, half)
+        elif step == 5:
+            ref = place(k, across, far, part)
+        else:
+            ref = place(k, across, far + part, half - part)
         return remote(ref, ref, send, recv, mate, lon)
 
     def halo(n):
@@ -168,27 +178,28 @@
         for n in range(4):
             halo(n).start()
 
-    halo(5).start()
     if spread:
-        for k in (2, 3):
+        for k in merge_items:
             hop(k, 1).start()
             hop(k, 0).start()
 
         def pass_on(k):
             hop(k, 1).wait_recv()
-            hop(k, 2).start()
-            hop(k, 3).start()
+            for step in (2, 3, 4):
+                hop(k, step).start()
 
         def pass_far(k):
-            hop(k, 2).wait_recv()
-            hop(k, 4).start()
+            for step in (2, 3):
+                hop(k, step).wait_recv()
+                hop(k, step + 3).start()
 
         def arrived(k):
-            for step in (0, 3, 4):
+            for step in (0, 4, 5, 6):
                 hop(k, step).wait_recv()
 
         pass_on(0)
         pass_on(1)
+        halo(5).start()
         pass_far(0)
         pass_far(1)
         own[0].wait()
@@ -196,6 +207,7 @@
         arrived(0)
         arrived(1)
     else:
+        halo(5).start()
         own[0].wait()
         own[1].wait()
 
@@ -255,6 +267,7 @@
         @pl.when(w == 3)
         def _():
             if spread:
+                pass_on(4)
                 pass_far(3)
             local[5].wait()
             halo(5).wait_recv()
@@ -317,20 +330,22 @@
         weight = w_merge[pl.ds(pl.multiple_of(shard * width, width), width), :]
         return jnp.dot(merge_in[shard], weight, preferred_element_type=jnp.float32)
 
+    for k in merge_items:
+        own[k].wait()
     if spread:
-        own[2].wait()
-        own[3].wait()
+        pass_on(5)
+        pass_far(4)
         total = product(lat)
-        hop(2, 0).wait_recv()
-        hop(3, 0).wait_recv()
+        pass_far(5)
+        for k in merge_items:
+            hop(k, 0).wait_recv()
         total = total + product(mate)
         total = total + product(across)
-        for k in (2, 3):
-            hop(k, 3).wait_recv()
-            hop(k, 4).wait_recv()
+        for k in merge_items:
+            for step in (4, 5, 6):
+                hop(k, step).wait_recv()
         total = total + product(across_mate)
     else:
-        own[2].wait()
         total = sum(product(n) for n in range(4))
     count = WIN * WIN // 4
     for w in range(4):
@@ -338,8 +353,8 @@
         out[w // 2, :, w % 2] = piece.astype(out.dtype)
 
     if spread:
-        for k in range(4):
-            for step in range(5):
+        for k in range(len(items)):
+            for step in range(7):
                 hop(k, step).wait_send()
     halo(4).wait_send()
     halo(5).wait_send()
@@ -362,8 +377,10 @@
     n_lat = lax.axis_size("lat")
     spread = (
         n_lat == 4
+        and lax.axis_size("lon") % 4 == 0
         and merge_weight.shape[0] == width
         and all(w.shape[0] % 32 == 0 for w in (inproj_weight, outproj_weight))
+        and width % (64 * CHUNKS) == 0
     )
     if not spread:
         inproj_weight, outproj_weight, merge_weight = (
@@ -397,12 +414,12 @@
             pltpu.SemaphoreType.DMA((6,)),
             pltpu.SemaphoreType.DMA((8,)),
             pltpu.SemaphoreType.DMA((8,)),
-            pltpu.SemaphoreType.DMA((4,)),
-            pltpu.SemaphoreType.DMA((4, 5)),
-            pltpu.SemaphoreType.DMA((4, 5)),
+            pltpu.SemaphoreType.DMA((2 + CHUNKS,)),
+            pltpu.SemaphoreType.DMA((2 + CHUNKS, 7)),
+            pltpu.SemaphoreType.DMA((2 + CHUNKS, 7)),
         ],
         compiler_params=pltpu.CompilerParams(
-            collective_id=0, has_side_effects=True, vmem_limit_bytes=48 * 1024 * 1024
+            collective_id=0, has_side_effects=True, vmem_limit_bytes=67043328
         ),
         name="window_attention_merge",
     )(

time: 58.8 us -> 46.4 us (0.79)
  the two profiles are of different devices: /device:TPU:27 before, /device:TPU:0 now
where the time goes in v2:
time: 46.4 us; the launch traced here: 45.9 us
  Pallas kernels  42.8 us (92%)
  local copies, waits for them, and re-layouts  3.03 us (7%)
    pallas_call x1, Pallas kernels, per_device(): pl.pallas_call(functools.partial(kernel, spread), out_shape=jax.ShapeDtyp...  42.8 us
    unnamed x1, local copies, waits for them, and re-layouts  1.77 us
    reshape x1, local copies, waits for them, and re-layouts, per_device(): norm_gain.reshape(1, width)  1.27 us

profile of v2, /device:TPU:0, one launch (start us, length us, event | category | flops | bytes accessed | tf_op | source)
XLA Modules:
  0.0 45.9 jit_solution(10173051808546632108)
XLA Ops:
  0.0 1.3 %reshape.13.norm_gain = f32[1,768]{1,0:T(1,128)} reshape(f32[768]{0:T(1024)} %param.9) | data formatting | bytes 6144 | tf_op jit(solution)/shard_map/reshape | solution.py:427
  1.3 42.8 %window_attention_merge.1 = bf16[2,8,2,8,768]{4,3,2,1,0:T(8,128)(2,1)} custom-call(bf16[32,4,8,768]{3,2,1,0:T(8,128)(2,1)} %bitcast.3, f32[1,768]{1,0:T(1,128)} %reshape.13.norm_gain, bf16[192,1152]{1,0:T(8,128)(2,1)} %in_shard.1, bf16[96,768]{1,0:T(8,128)(2,1)} %out_shard.1, f32[4,1,768]{2,1,0:T(1,128)} %bitcast.5, bf16[768,768]{1,0:T(8,128)(2,1)} %merge_shard.1, ...), custom_call_target="tpu_custom_call" | custom-call | tf_op jit(solution)/shard_map/window_attention_merge/pallas_call | solution.py:398
  44.1 1.8 %copy.10 = bf16[16,16,768]{2,1,0:T(8,128)(2,1)} copy(bf16[16,16,768]{2,1,0:T(8,128)(2,1)} %bitcast.4) | data formatting | bytes 786432
